TPU v7x, 32 devices: a whole 2x2x4 slice. The times are simulated.
32 devices in a mesh: group: 2 (over x), context: 16 (over z, y, core).
Axes of the slice: x: 2, y: 2, z: 4, core: 2. Of those that a mesh axis runs over, the one named last changes fastest.
Arguments:
- features: bfloat16 [4096, 3, 8192], P(('group', 'context')), parts along dimension 0, may hold values from -6 to 6
- base_rows: bfloat16 [4, 3, 8192], replicated, may hold values from -6 to 6
- positions: int32 [128], P('group'), parts along dimension 0, may hold values from 0 to 2047, as said below
- alt_bases: int32 [128], P('group'), parts along dimension 0, may hold values from 0 to 3
- decay_rate: float32 [16, 8192], replicated, may hold values from 9.765625e-06 to 0.03
- residue: float32 [16, 8192], replicated, may hold values from -5 to 5
- skip_gain: float32 [8192], replicated, may hold values from 0.5 to 1.5
Outputs:
- ref_out: bfloat16 [4096, 8192], P(('group', 'context')), parts along dimension 0
- effect: bfloat16 [4096, 8192], P(('group', 'context')), parts along dimension 0
- channel_score: float32 [16384], P(('group', 'context')), parts along dimension 0
There are 2 independent parts, one for each index of `group`. A program takes and returns all parts, laid end to end along the dimension named above; an argument that names none is the same for every part. Nothing has to cross between parts.
Inputs may be any that keep to these rules, and one draw needn't show every extreme that they name: `positions`: ascending; exactly one lies in each aligned stretch of 32 positions; the first is 0 and the last is 2047. `alt_bases`: an index into the first dimension of base_rows.
All inputs are finite; a program needn't handle non-finite values.
Results may differ from a plain program's by a relative error of at most 0.0005.
Values may be sent and summed in bfloat16 or wider, within the bound.
A program may use at most 384 MiB of HBM per device.

v0:
```python
import functools

import jax
import jax.numpy as jnp
import numpy as np
from jax import lax
from jax.experimental import pallas as pl
from jax.experimental.pallas import tpu as pltpu
from jax.sharding import PartitionSpec as P

F32 = jnp.float32
BF16 = jnp.bfloat16
RATE_MAX = 0.03
KD = 10
KB = 7


def cheb_table(length):
    nodes = 64
    theta = (np.arange(nodes) + 0.5) * np.pi / nodes
    rate = (np.cos(theta) + 1.0) * (RATE_MAX / 2)
    values = np.exp(-rate[None] * np.arange(length)[:, None])
    basis = np.cos(np.arange(16)[:, None] * theta[None])
    table = 2.0 / nodes * values @ basis.T
    table[:, 0] *= 0.5
    return table


def split3_lhs(a):
    a = a.astype(np.float32)
    hi = a.astype(jnp.bfloat16)
    lo = (a - hi.astype(np.float32)).astype(jnp.bfloat16)
    return np.concatenate([hi, lo, hi], axis=1)


def split3_rhs(x):
    hi = x.astype(BF16)
    lo = (x - hi.astype(F32)).astype(BF16)
    return jnp.concatenate([hi, hi, lo], axis=0)


def pad_rows(a, rows):
    return np.concatenate([a, np.zeros((rows - a.shape[0],) + a.shape[1:])], axis=0)


def pad_cols(a, cols):
    return np.concatenate([a, np.zeros((a.shape[0], cols - a.shape[1]))], axis=1)


def cheb_terms(rate, count):
    x = rate * (2.0 / RATE_MAX) - 1.0
    terms = [jnp.ones_like(x), x]
    while len(terms) < count:
        terms.append(2.0 * x * terms[-1] - terms[-2])
    return terms


def modal_coef(rate, residue):
    z = 2.0 * rate
    tail = 1.0 - z * (1.0 / 2) * (1.0 - z * (1.0 / 3) * (1.0 - z * (1.0 / 4) * (1.0 - z * (1.0 / 5) * (1.0 - z * (1.0 / 6)))))
    return residue * jnp.sqrt(z * tail)


def moments_kernel(nv, where_ref, alt_ref, gm_ref, k_ref, v_ref, base_ref, out_ref):
    forcing = k_ref[0].astype(F32) * v_ref[0].astype(F32)
    length = forcing.shape[0]
    stretch = length // nv
    moments = jnp.dot(gm_ref[...], split3_rhs(forcing), preferred_element_type=F32)
    table = base_ref[1].astype(F32) * base_ref[2].astype(F32)
    rows = [moments[:KD]]
    step = lax.broadcasted_iota(jnp.int32, (stretch, 1), 0)
    pick = lax.broadcasted_iota(jnp.int32, (table.shape[0], 1), 0)
    for i in range(nv):
        new = jnp.sum(jnp.where(pick == alt_ref[i], table, 0.0), axis=0, keepdims=True)
        part = forcing[i * stretch : (i + 1) * stretch]
        old = jnp.sum(jnp.where(step == where_ref[i], part, 0.0), axis=0, keepdims=True)
        rows.append(new - old)
    rows.append(jnp.zeros((out_ref.shape[1] - KD - nv, forcing.shape[1]), F32))
    packed = jnp.concatenate(rows, axis=0)
    width = out_ref.shape[2]
    for d in range(out_ref.shape[0]):
        out_ref[d] = packed[:, d * width : (d + 1) * width]


def combine_kernel(nv, length, lag_ref, in_ref, rate_ref, residue_ref, out_ref):
    devices = in_ref.shape[0]
    rate = rate_ref[...]
    terms = cheb_terms(rate, KD)
    lead = modal_coef(rate, residue_ref[...]) * jnp.exp(-rate)
    leads = [lead * term for term in terms]
    moments = [in_ref[:, k, :] for k in range(KD)]
    subs = [in_ref[:, KD + i, :] for i in range(nv)]
    lags = [lag_ref[i] for i in range(nv)]
    row = lax.broadcasted_iota(jnp.int32, (devices, in_ref.shape[2]), 0)
    base = [jnp.zeros((devices, in_ref.shape[2]), F32) for _ in range(KD)]
    change = [jnp.zeros((devices, in_ref.shape[2]), F32) for _ in range(KD)]

    def before(ends, rate_n):
        ends = jnp.where(row >= 1, pltpu.roll(ends, 1, 0), 0.0)
        hop = 1
        while hop < devices:
            fade = jnp.exp(rate_n * (-float(length) * hop))
            ends = ends + fade * jnp.where(row >= hop, pltpu.roll(ends, hop, 0), 0.0)
            hop *= 2
        return ends

    for n in range(rate.shape[0]):
        rate_n = rate[n : n + 1]
        ends = terms[0][n : n + 1] * moments[0]
        for k in range(1, KD):
            ends = ends + terms[k][n : n + 1] * moments[k]
        shifted = jnp.exp(-rate_n * lags[0]) * subs[0]
        for i in range(1, nv):
            shifted = shifted + jnp.exp(-rate_n * lags[i]) * subs[i]
        ends, shifted = before(ends, rate_n), before(shifted, rate_n)
        for k in range(KD):
            base[k] = base[k] + leads[k][n : n + 1] * ends
            change[k] = change[k] + leads[k][n : n + 1] * shifted
    for k in range(KD):
        out_ref[:, k, :] = base[k]
        out_ref[:, KD + k, :] = change[k]
    for k in range(2 * KD, out_ref.shape[1]):
        out_ref[:, k, :] = jnp.zeros((devices, in_ref.shape[2]), F32)


def finish_kernel(
    nv, where_ref, alt_ref, gb_ref, gx_ref, gd_ref, q_ref, k_ref, v_ref, base_ref, rate_ref, residue_ref,
    skip_ref, enter_ref, out_ref, effect_ref, score_ref, pad_ref,
):
    length, width = q_ref.shape[1:]
    half, stretch = length // 2, length // nv
    q = q_ref[0].astype(F32)
    forcing = k_ref[0].astype(F32) * v_ref[0].astype(F32)
    skip = skip_ref[...]
    rate = rate_ref[...]
    terms = cheb_terms(rate, KD)
    coef = modal_coef(rate, residue_ref[...])
    lead = coef * jnp.exp(-rate)
    weights = [jnp.sum(coef * term, axis=0, keepdims=True) for term in terms]
    entering = jnp.concatenate([enter_ref[d] for d in range(enter_ref.shape[0])], axis=1)

    filtered = []
    for b in range(2):
        products = jnp.dot(
            gb_ref[...], split3_rhs(forcing[b * half : (b + 1) * half]), preferred_element_type=F32
        )
        total = weights[0] * products[:half]
        for k in range(1, KB):
            total = total + weights[k] * products[k * half : (k + 1) * half]
        filtered.append(total)
        if b == 0:
            first = products[KB * half : KB * half + KB]
    state = terms[0] * first[0:1]
    for k in range(1, KB):
        state = state + terms[k] * first[k : k + 1]
    state = lead * state
    cross = [jnp.sum(terms[k] * state, axis=0, keepdims=True) for k in range(KB)]
    zeros = jnp.zeros((16, width), F32)
    z = jnp.concatenate([entering[:KD], zeros[: 16 - KD]] + cross + [zeros[: 16 - KB]], axis=0)
    filtered = jnp.concatenate(filtered, axis=0) + jnp.dot(
        gx_ref[...], split3_rhs(z), preferred_element_type=F32
    )
    inner = filtered + skip * forcing
    out_ref[...] = (q * inner).astype(out_ref.dtype)

    z = jnp.concatenate([entering[KD : 2 * KD], zeros[: 16 - KD]], axis=0)
    delta = jnp.dot(gd_ref[...], split3_rhs(z), preferred_element_type=F32)
    z = jnp.concatenate(weights + [zeros[: 16 - KD]], axis=0)
    impulse = jnp.dot(gd_ref[...], split3_rhs(z), preferred_element_type=F32)
    for c in range(width // 128):
        pad_ref[c, :length, :] = jnp.zeros((length, 128), F32)
        pad_ref[c, length:, :] = impulse[:, c * 128 : (c + 1) * 128]
    table = base_ref[...].astype(F32)
    step = lax.broadcasted_iota(jnp.int32, (stretch, 1), 0)
    pick = lax.broadcasted_iota(jnp.int32, (table.shape[1], 1), 0)
    deltas = [delta[i * stretch : (i + 1) * stretch] for i in range(nv)]
    total = jnp.zeros((1, width), F32)
    for i in range(nv):
        rows = slice(i * stretch, (i + 1) * stretch)
        hit = step == where_ref[i]
        chosen = pick == alt_ref[i]
        new_q, new_k, new_v = (jnp.sum(jnp.where(chosen, table[j], 0.0), axis=0, keepdims=True) for j in range(3))
        force_step = jnp.where(hit, new_k * new_v - forcing[rows], 0.0)
        gate_step = jnp.where(hit, new_q - q[rows], 0.0)
        impact = jnp.sum(force_step, axis=0, keepdims=True)
        place = where_ref[i]
        for j in range(i, nv):
            response = jnp.concatenate(
                [
                    pad_ref[c, pl.ds(length + (j - i) * stretch - place, stretch), :]
                    for c in range(width // 128)
                ],
                axis=1,
            )
            deltas[j] = deltas[j] + response * impact
        change = (q[rows] + gate_step) * (deltas[i] + skip * force_step) + gate_step * inner[rows]
        effect_ref[rows, :] = change.astype(effect_ref.dtype)
        total = total + jnp.sum(change, axis=0, keepdims=True)
    score_ref[...] = total


def exchange(blocks):
    return lax.all_to_all(blocks, "context", 0, 0, tiled=True)


def on_device(features, base_rows, positions, alt_bases, decay_rate, residue, skip_gain):
    length, _, width = features.shape
    modes = decay_rate.shape[0]
    devices = lax.axis_size("context")
    me = lax.axis_index("context")
    nv = positions.shape[0] // devices
    share = width // devices
    half, stretch = length // 2, length // nv
    table = cheb_table(length)

    rows = features.transpose(1, 0, 2)
    bases = base_rows.transpose(1, 0, 2)
    local = positions.reshape(devices, nv) - jnp.arange(devices, dtype=jnp.int32)[:, None] * length
    within = local - jnp.arange(nv, dtype=jnp.int32)[None] * stretch
    my_within = lax.dynamic_index_in_dim(within, me, 0, keepdims=False)
    my_alt = lax.dynamic_slice_in_dim(alt_bases, me * nv, nv)
    lags = (length - 1 - local).astype(F32).T
    lags = jnp.broadcast_to(lags[:, :, None], (nv, devices, 128))

    smem = pl.BlockSpec(memory_space=pltpu.SMEM)
    parallel = pltpu.CompilerParams(dimension_semantics=("arbitrary",))

    def row_spec(index, chunk):
        return pl.BlockSpec((1, length, chunk), lambda j, index=index: (index, 0, j))

    def whole(a):
        return pl.BlockSpec(a.shape, lambda j: (0,) * a.ndim)

    gm = jnp.asarray(split3_lhs(pad_rows(table[::-1, :KD].T, 16)))
    chunk = 1024
    sends = pl.pallas_call(
        functools.partial(moments_kernel, nv),
        grid=(width // chunk,),
        in_specs=[
            smem, smem, whole(gm), row_spec(1, chunk), row_spec(2, chunk),
            pl.BlockSpec((3, bases.shape[1], chunk), lambda j: (0, 0, j)),
        ],
        out_specs=pl.BlockSpec((chunk // share, 16, share), lambda j: (j, 0, 0)),
        out_shape=jax.ShapeDtypeStruct((devices, 16, share), F32),
        compiler_params=parallel,
        name="moments",
    )(my_within, my_alt, gm, rows, rows, bases)

    got = exchange(sends)
    my_rate = lax.dynamic_slice_in_dim(decay_rate, me * share, share, axis=1)
    my_residue = lax.dynamic_slice_in_dim(residue, me * share, share, axis=1)
    back = pl.pallas_call(
        functools.partial(combine_kernel, nv, length),
        grid=(share // 128,),
        in_specs=[
            whole(lags),
            pl.BlockSpec((devices, 16, 128), lambda j: (0, 0, j)),
            pl.BlockSpec((modes, 128), lambda j: (0, j)),
            pl.BlockSpec((modes, 128), lambda j: (0, j)),
        ],
        out_specs=pl.BlockSpec((devices, 24, 128), lambda j: (0, 0, j)),
        out_shape=jax.ShapeDtypeStruct((devices, 24, share), F32),
        compiler_params=parallel,
        name="combine",
    )(lags, got, my_rate, my_residue)
    entering = exchange(back)

    lag = np.arange(half)[:, None] - np.arange(half)[None]
    toeplitz = np.where((lag >= 0)[None], table[np.maximum(lag, 0), :KB].transpose(2, 0, 1), 0.0)
    toeplitz = toeplitz.reshape(KB * half, half)
    ends = pad_rows(table[:half, :KB][::-1].T, 8)
    gb = jnp.asarray(split3_lhs(np.concatenate([toeplitz, ends], axis=0)))
    late = np.concatenate([np.zeros((half, 16)), pad_cols(table[:half, :KB], 16)], axis=0)
    gx = jnp.asarray(split3_lhs(np.concatenate([pad_cols(table[:, :KD], 16), late], axis=1)))
    gd = jnp.asarray(split3_lhs(pad_cols(table[:, :KD], 16)))
    chunk = 512
    ref_out, effect, score_part = pl.pallas_call(
        functools.partial(finish_kernel, nv),
        grid=(width // chunk,),
        in_specs=[
            smem, smem, whole(gb), whole(gx), whole(gd),
            row_spec(0, chunk), row_spec(1, chunk), row_spec(2, chunk),
            pl.BlockSpec((3, bases.shape[1], chunk), lambda j: (0, 0, j)),
            pl.BlockSpec((modes, chunk), lambda j: (0, j)),
            pl.BlockSpec((modes, chunk), lambda j: (0, j)),
            pl.BlockSpec((1, chunk), lambda j: (0, j)),
            pl.BlockSpec((chunk // share, 24, share), lambda j: (j, 0, 0)),
        ],
        out_specs=[
            pl.BlockSpec((length, chunk), lambda j: (0, j)),
            pl.BlockSpec((length, chunk), lambda j: (0, j)),
            pl.BlockSpec((1, chunk), lambda j: (0, j)),
        ],
        out_shape=[
            jax.ShapeDtypeStruct((length, width), BF16),
            jax.ShapeDtypeStruct((length, width), BF16),
            jax.ShapeDtypeStruct((1, width), F32),
        ],
        scratch_shapes=[pltpu.VMEM((chunk // 128, 2 * length, 128), F32)],
        compiler_params=parallel,
        name="finish",
    )(
        my_within, my_alt, gb, gx, gd, rows, rows, rows, bases, decay_rate, residue,
        skip_gain.reshape(1, width), entering,
    )
    channel_score = lax.psum_scatter(score_part[0], "context", scatter_dimension=0, tiled=True)
    return ref_out, effect, channel_score


def solution(mesh):
    return jax.shard_map(
        on_device,
        mesh=mesh,
        in_specs=(P(("group", "context"), None, None), P(), P("group"), P("group"), P(), P(), P()),
        out_specs=(
            P(("group", "context"), None),
            P(("group", "context"), None),
            P(("group", "context")),
        ),
        check_vma=False,
    )
```

profile of v0, /device:TPU:0, one launch (start us, length us, event | category | flops | bytes accessed | tf_op | source)
XLA Modules:
  0.0 140.6 jit_solution(2306512676773285710)
XLA Ops:
  0.7 0.7 reshape.23
  1.4 1.3 dynamic_slice.14.alt_ref
  2.7 0.1 convert_bitcast_fusion
  2.8 0.5 fusion.1.where_ref
  3.3 6.6 %moments.1 = f32[16,16,512]{2,1,0:T(8,128)} custom-call(s32[4]{0:T(128)} %fusion.1.where_ref, s32[4]{0:T(128)} %dynamic_slice.14.alt_ref, bf16[16,384]{1,0:T(8,128)(2,1)} %constant.33.clone.gm_ref, bf16[3,128,8192]{2,1,0:T(8,128)(2,1)} %bitcast.9, bf16[3,128,8192]{2,1,0:T(8,128)(2,1)} %bitcast.10, bf16[3,4,8192]{2,1,0:T(4,128)(2,1)} %bitcast.14), custom_call_target="tpu_custom_call" | custom-call | tf_op jit(solution)/shard_map/moments/pallas_call | solution.py:236
  9.9 0.0 copy-start.2
  9.9 7.5 %all-to-all-start = ((f32[16,16,512]{2,1,0:T(8,128)}), f32[16,16,512]{2,1,0:T(8,128)S(1)}, u32[]{:S(2)}, u32[]{:S(2)}) async-start(f32[16,16,512]{2,1,0:T(8,128)} %moments.1), calls=%async_computation | async-start | bytes 1048576 | tf_op jit(solution)/shard_map/all_to_all | solution.py:203
  17.5 0.1 copy.16
  17.5 1.4 constant_dynamic-slice_fusion
  18.9 12.8 %all-to-all-done.in_ref = f32[16,16,512]{2,1,0:T(8,128)S(1)} async-done(((f32[16,16,512]{2,1,0:T(8,128)}), f32[16,16,512]{2,1,0:T(8,128)S(1)}, u32[]{:S(2)}, u32[]{:S(2)}) %all-to-all-start) | async-done | bytes 524320 | tf_op jit(solution)/shard_map/all_to_all | solution.py:203
  31.7 0.0 copy-start.1
  31.7 0.8 broadcast_in_dim.2.lag_ref
  32.5 0.0 copy-done.1
  32.5 4.8 %combine.1 = f32[16,24,512]{2,1,0:T(8,128)} custom-call(f32[4,16,128]{2,1,0:T(8,128)} %broadcast_in_dim.2.lag_ref, f32[16,16,512]{2,1,0:T(8,128)} %copy-done.1, f32[16,512]{1,0:T(8,128)} %get-tuple-element.12.rate_ref, f32[16,512]{1,0:T(8,128)} %get-tuple-element.11.residue_ref), custom_call_target="tpu_custom_call" | custom-call | tf_op jit(solution)/shard_map/combine/pallas_call | solution.py:252
  37.3 4.2 %all-to-all-start.1 = ((f32[16,24,512]{2,1,0:T(8,128)}), f32[16,24,512]{2,1,0:T(8,128)S(1)}, u32[]{:S(2)}, u32[]{:S(2)}) async-start(f32[16,24,512]{2,1,0:T(8,128)} %combine.1), calls=%async_computation.1 | async-start | bytes 1572864 | tf_op jit(solution)/shard_map/all_to_all | solution.py:203
  41.5 0.0 copy-done.2
  41.5 0.6 dynamic-slice
  42.8 17.4 %all-to-all-done.1.enter_ref = f32[16,24,512]{2,1,0:T(8,128)S(1)} async-done(((f32[16,24,512]{2,1,0:T(8,128)}), f32[16,24,512]{2,1,0:T(8,128)S(1)}, u32[]{:S(2)}, u32[]{:S(2)}) %all-to-all-start.1) | async-done | bytes 786464 | tf_op jit(solution)/shard_map/all_to_all | solution.py:203
  60.2 0.0 copy-start
  60.2 0.9 copy-done
  61.1 17.3 %finish.1 = (bf16[128,8192]{1,0:T(8,128)(2,1)}, bf16[128,8192]{1,0:T(8,128)(2,1)}, f32[1,8192]{1,0:T(1,128)}) custom-call(s32[4]{0:T(128)} %fusion.1.where_ref, s32[4]{0:T(128)} %dynamic_slice.14.alt_ref, bf16[456,192]{1,0:T(8,128)(2,1)} %constant.34.clone.gb_ref, bf16[128,96]{1,0:T(8,128)(2,1)} %constant.35.clone.gx_ref, ...), custom_call_target="tpu_custom_call" | custom-call | tf_op jit(solution)/shard_map/finish/pallas_call | solution.py:277
  78.3 61.6 %all-reduce = f32[8192]{0:T(1024)S(1)} all-reduce(f32[8192]{0:T(1024)} %bitcast.17), channel_id=2, replica_groups=mesh['group'=2,'context'=16] {'context'}, use_global_device_ids=true, to_apply=%region_0.1.clone | all-reduce | flops 8192 | bytes 65536
  139.9 0.7 dynamic-slice.1
  (2 shorter events, 0.0 us)
Async XLA Ops:
  9.9 31.6 %copy-start.2 = (u32[32]{0:T(128)S(1)}, u32[32]{0:T(128)}, u32[]{:S(2)}) copy-start(u32[32]{0:T(128)} %constant.39) | copy-start | bytes 388
  9.9 21.8 %all-to-all-start = ((f32[16,16,512]{2,1,0:T(8,128)}), f32[16,16,512]{2,1,0:T(8,128)S(1)}, u32[]{:S(2)}, u32[]{:S(2)}) async-start(f32[16,16,512]{2,1,0:T(8,128)} %moments.1), calls=%async_computation | async-start | bytes 1048576 | tf_op jit(solution)/shard_map/all_to_all | solution.py:203
  31.7 0.8 copy-start.1
  37.3 22.8 %all-to-all-start.1 = ((f32[16,24,512]{2,1,0:T(8,128)}), f32[16,24,512]{2,1,0:T(8,128)S(1)}, u32[]{:S(2)}, u32[]{:S(2)}) async-start(f32[16,24,512]{2,1,0:T(8,128)} %combine.1), calls=%async_computation.1 | async-start | bytes 1572864 | tf_op jit(solution)/shard_map/all_to_all | solution.py:203
  60.2 0.9 copy-start
where the time goes:
time: 142 us; the launch traced here: 141 us
  blocking collectives  61.6 us (43%)
  waiting for transfers between devices  30.2 us (21%)
  Pallas kernels  28.7 us (20%)
  starting transfers between devices  11.7 us (8%)
  local copies, waits for them, and re-layouts  6.44 us (5%)
    unnamed x1, blocking collectives  61.6 us
    all_to_all x2, waiting for transfers between devices, exchange(): return lax.all_to_all(blocks, 'context', 0, 0, tiled=True)  30.2 us
    pallas_call x1, Pallas kernels, on_device(): pl.pallas_call(functools.partial(finish_kernel, nv), grid=(width // chunk...  17.3 us
    all_to_all x2, starting transfers between devices, exchange(): return lax.all_to_all(blocks, 'context', 0, 0, tiled=True)  11.7 us
    pallas_call x1, Pallas kernels, on_device(): pl.pallas_call(functools.partial(moments_kernel, nv), grid=(width // chun...  6.61 us
    pallas_call x1, Pallas kernels, on_device(): pl.pallas_call(functools.partial(combine_kernel, nv, length), grid=(share...  4.79 us
  transfers between devices with their start and end apart: 2, of which 2 were waited for; matrix products, arithmetic and copies ran while one was open for 1% of the time, Pallas kernels for 0%

commit v1 on v0

--- a/solution.py
+++ b/solution.py
@@ -10,6 +10,7 @@
 
 F32 = jnp.float32
 BF16 = jnp.bfloat16
+MESH = pl.DeviceIdType.MESH
 RATE_MAX = 0.03
 KD = 10
 KB = 7
@@ -75,25 +76,19 @@
         part = forcing[i * stretch : (i + 1) * stretch]
         old = jnp.sum(jnp.where(step == where_ref[i], part, 0.0), axis=0, keepdims=True)
         rows.append(new - old)
-    rows.append(jnp.zeros((out_ref.shape[1] - KD - nv, forcing.shape[1]), F32))
     packed = jnp.concatenate(rows, axis=0)
-    width = out_ref.shape[2]
+    height = packed.shape[0]
+    tiles = out_ref.shape[1] // height
     for d in range(out_ref.shape[0]):
-        out_ref[d] = packed[:, d * width : (d + 1) * width]
-
-
-def combine_kernel(nv, length, lag_ref, in_ref, rate_ref, residue_ref, out_ref):
+        for c in range(tiles):
+            lanes = (d * tiles + c) * 128
+            out_ref[d, c * height : (c + 1) * height, :] = packed[:, lanes : lanes + 128]
+
+
+def combine(nv, length, lag_ref, in_ref, rate_ref, residue_ref, out_ref):
     devices = in_ref.shape[0]
-    rate = rate_ref[...]
-    terms = cheb_terms(rate, KD)
-    lead = modal_coef(rate, residue_ref[...]) * jnp.exp(-rate)
-    leads = [lead * term for term in terms]
-    moments = [in_ref[:, k, :] for k in range(KD)]
-    subs = [in_ref[:, KD + i, :] for i in range(nv)]
-    lags = [lag_ref[i] for i in range(nv)]
-    row = lax.broadcasted_iota(jnp.int32, (devices, in_ref.shape[2]), 0)
-    base = [jnp.zeros((devices, in_ref.shape[2]), F32) for _ in range(KD)]
-    change = [jnp.zeros((devices, in_ref.shape[2]), F32) for _ in range(KD)]
+    height = KD + nv
+    row = lax.broadcasted_iota(jnp.int32, (devices, 128), 0)
 
     def before(ends, rate_n):
         ends = jnp.where(row >= 1, pltpu.roll(ends, 1, 0), 0.0)
@@ -104,23 +99,82 @@
             hop *= 2
         return ends
 
-    for n in range(rate.shape[0]):
-        rate_n = rate[n : n + 1]
-        ends = terms[0][n : n + 1] * moments[0]
-        for k in range(1, KD):
-            ends = ends + terms[k][n : n + 1] * moments[k]
-        shifted = jnp.exp(-rate_n * lags[0]) * subs[0]
-        for i in range(1, nv):
-            shifted = shifted + jnp.exp(-rate_n * lags[i]) * subs[i]
-        ends, shifted = before(ends, rate_n), before(shifted, rate_n)
+    for c in range(rate_ref.shape[1] // 128):
+        rate = rate_ref[:, c * 128 : (c + 1) * 128]
+        terms = cheb_terms(rate, KD)
+        lead = modal_coef(rate, residue_ref[:, c * 128 : (c + 1) * 128]) * jnp.exp(-rate)
+        leads = [lead * term for term in terms]
+        moments = [in_ref[:, c * height + k, :] for k in range(KD)]
+        subs = [in_ref[:, c * height + KD + i, :] for i in range(nv)]
+        lags = [lag_ref[i] for i in range(nv)]
+        base = [jnp.zeros((devices, 128), F32) for _ in range(KD)]
+        change = [jnp.zeros((devices, 128), F32) for _ in range(KD)]
+        for n in range(rate.shape[0]):
+            rate_n = rate[n : n + 1]
+            ends = terms[0][n : n + 1] * moments[0]
+            for k in range(1, KD):
+                ends = ends + terms[k][n : n + 1] * moments[k]
+            shifted = jnp.exp(-rate_n * lags[0]) * subs[0]
+            for i in range(1, nv):
+                shifted = shifted + jnp.exp(-rate_n * lags[i]) * subs[i]
+            ends, shifted = before(ends, rate_n), before(shifted, rate_n)
+            for k in range(KD):
+                base[k] = base[k] + leads[k][n : n + 1] * ends
+                change[k] = change[k] + leads[k][n : n + 1] * shifted
         for k in range(KD):
-            base[k] = base[k] + leads[k][n : n + 1] * ends
-            change[k] = change[k] + leads[k][n : n + 1] * shifted
-    for k in range(KD):
-        out_ref[:, k, :] = base[k]
-        out_ref[:, KD + k, :] = change[k]
-    for k in range(2 * KD, out_ref.shape[1]):
-        out_ref[:, k, :] = jnp.zeros((devices, in_ref.shape[2]), F32)
+            out_ref[:, c * 2 * KD + k, :] = base[k]
+            out_ref[:, c * 2 * KD + KD + k, :] = change[k]
+
+
+def greet(devices):
+    me = lax.axis_index("context")
+    barrier = pltpu.get_barrier_semaphore()
+    for hop in range(1, devices):
+        pl.semaphore_signal(
+            barrier, inc=1, device_id={"context": lax.rem(me + hop, devices)}, device_id_type=MESH
+        )
+    pl.semaphore_wait(barrier, devices - 1)
+
+
+def hand_out(src_ref, dst_ref, own_sem, send_sems, recv_sems):
+    devices = src_ref.shape[0]
+    me = lax.axis_index("context")
+    copies = []
+    for hop in range(1, devices):
+        peer = lax.rem(me + hop, devices)
+        copies.append(
+            pltpu.make_async_remote_copy(
+                src_ref=src_ref.at[peer],
+                dst_ref=dst_ref.at[me],
+                send_sem=send_sems.at[hop],
+                recv_sem=recv_sems.at[hop],
+                device_id={"context": peer},
+                device_id_type=MESH,
+            )
+        )
+        copies[-1].start()
+    own = pltpu.make_async_copy(src_ref.at[me], dst_ref.at[me], own_sem)
+    own.start()
+    return copies + [own]
+
+
+def route_kernel(
+    nv, length, lag_ref, mine_ref, rate_ref, residue_ref, out_ref,
+    got_ref, back_ref, own_sems, send_sems, recv_sems,
+):
+    greet(mine_ref.shape[0])
+    for copy in hand_out(mine_ref, got_ref, own_sems.at[0], send_sems.at[0], recv_sems.at[0]):
+        copy.wait()
+    combine(nv, length, lag_ref, got_ref, rate_ref, residue_ref, back_ref)
+    for copy in hand_out(back_ref, out_ref, own_sems.at[1], send_sems.at[1], recv_sems.at[1]):
+        copy.wait()
+
+
+def score_kernel(parts_ref, out_ref, got_ref, own_sem, send_sems, recv_sems):
+    greet(parts_ref.shape[0])
+    for copy in hand_out(parts_ref, got_ref, own_sem, send_sems, recv_sems):
+        copy.wait()
+    out_ref[...] = jnp.sum(got_ref[...], axis=0)
 
 
 def finish_kernel(
@@ -137,7 +191,14 @@
     coef = modal_coef(rate, residue_ref[...])
     lead = coef * jnp.exp(-rate)
     weights = [jnp.sum(coef * term, axis=0, keepdims=True) for term in terms]
-    entering = jnp.concatenate([enter_ref[d] for d in range(enter_ref.shape[0])], axis=1)
+    entering = jnp.concatenate(
+        [
+            enter_ref[d, c : c + 2 * KD, :]
+            for d in range(enter_ref.shape[0])
+            for c in range(0, enter_ref.shape[1], 2 * KD)
+        ],
+        axis=1,
+    )
 
     filtered = []
     for b in range(2):
@@ -199,10 +260,6 @@
     score_ref[...] = total
 
 
-def exchange(blocks):
-    return lax.all_to_all(blocks, "context", 0, 0, tiled=True)
-
-
 def on_device(features, base_rows, positions, alt_bases, decay_rate, residue, skip_gain):
     length, _, width = features.shape
     modes = decay_rate.shape[0]
@@ -210,6 +267,7 @@
     me = lax.axis_index("context")
     nv = positions.shape[0] // devices
     share = width // devices
+    tiles = share // 128
     half, stretch = length // 2, length // nv
     table = cheb_table(length)
 
@@ -240,30 +298,30 @@
             smem, smem, whole(gm), row_spec(1, chunk), row_spec(2, chunk),
             pl.BlockSpec((3, bases.shape[1], chunk), lambda j: (0, 0, j)),
         ],
-        out_specs=pl.BlockSpec((chunk // share, 16, share), lambda j: (j, 0, 0)),
-        out_shape=jax.ShapeDtypeStruct((devices, 16, share), F32),
+        out_specs=pl.BlockSpec((chunk // share, tiles * (KD + nv), 128), lambda j: (j, 0, 0)),
+        out_shape=jax.ShapeDtypeStruct((devices, tiles * (KD + nv), 128), F32),
         compiler_params=parallel,
         name="moments",
     )(my_within, my_alt, gm, rows, rows, bases)
 
-    got = exchange(sends)
     my_rate = lax.dynamic_slice_in_dim(decay_rate, me * share, share, axis=1)
     my_residue = lax.dynamic_slice_in_dim(residue, me * share, share, axis=1)
-    back = pl.pallas_call(
-        functools.partial(combine_kernel, nv, length),
-        grid=(share // 128,),
-        in_specs=[
-            whole(lags),
-            pl.BlockSpec((devices, 16, 128), lambda j: (0, 0, j)),
-            pl.BlockSpec((modes, 128), lambda j: (0, j)),
-            pl.BlockSpec((modes, 128), lambda j: (0, j)),
-        ],
-        out_specs=pl.BlockSpec((devices, 24, 128), lambda j: (0, 0, j)),
-        out_shape=jax.ShapeDtypeStruct((devices, 24, share), F32),
-        compiler_params=parallel,
-        name="combine",
-    )(lags, got, my_rate, my_residue)
-    entering = exchange(back)
+    vmem = pl.BlockSpec(memory_space=pltpu.VMEM)
+    entering = pl.pallas_call(
+        functools.partial(route_kernel, nv, length),
+        in_specs=[vmem] * 4,
+        out_specs=vmem,
+        out_shape=jax.ShapeDtypeStruct((devices, tiles * 2 * KD, 128), F32),
+        scratch_shapes=[
+            pltpu.VMEM((devices, tiles * (KD + nv), 128), F32),
+            pltpu.VMEM((devices, tiles * 2 * KD, 128), F32),
+            pltpu.SemaphoreType.DMA((2,)),
+            pltpu.SemaphoreType.DMA((2, devices)),
+            pltpu.SemaphoreType.DMA((2, devices)),
+        ],
+        compiler_params=pltpu.CompilerParams(collective_id=0, has_side_effects=True),
+        name="route",
+    )(lags, sends, my_rate, my_residue)
 
     lag = np.arange(half)[:, None] - np.arange(half)[None]
     toeplitz = np.where((lag >= 0)[None], table[np.maximum(lag, 0), :KB].transpose(2, 0, 1), 0.0)
@@ -284,7 +342,7 @@
             pl.BlockSpec((modes, chunk), lambda j: (0, j)),
             pl.BlockSpec((modes, chunk), lambda j: (0, j)),
             pl.BlockSpec((1, chunk), lambda j: (0, j)),
-            pl.BlockSpec((chunk // share, 24, share), lambda j: (j, 0, 0)),
+            pl.BlockSpec((chunk // share, tiles * 2 * KD, 128), lambda j: (j, 0, 0)),
         ],
         out_specs=[
             pl.BlockSpec((length, chunk), lambda j: (0, j)),
@@ -303,8 +361,21 @@
         my_within, my_alt, gb, gx, gd, rows, rows, rows, bases, decay_rate, residue,
         skip_gain.reshape(1, width), entering,
     )
-    channel_score = lax.psum_scatter(score_part[0], "context", scatter_dimension=0, tiled=True)
-    return ref_out, effect, channel_score
+    channel_score = pl.pallas_call(
+        score_kernel,
+        in_specs=[vmem],
+        out_specs=vmem,
+        out_shape=jax.ShapeDtypeStruct((tiles, 128), F32),
+        scratch_shapes=[
+            pltpu.VMEM((devices, tiles, 128), F32),
+            pltpu.SemaphoreType.DMA,
+            pltpu.SemaphoreType.DMA((devices,)),
+            pltpu.SemaphoreType.DMA((devices,)),
+        ],
+        compiler_params=pltpu.CompilerParams(collective_id=1, has_side_effects=True),
+        name="score",
+    )(score_part.reshape(devices, tiles, 128))
+    return ref_out, effect, channel_score.reshape(share)
 
 
 def solution(mesh):

time: 142 us -> 76.1 us (0.54)
  blocking collectives: 61.6 us -> 0 us
  Pallas kernels: 28.7 us -> 68.6 us
  waiting for transfers between devices: 30.2 us -> 0 us
  starting transfers between devices: 11.7 us -> 0 us
    unnamed x1 -> x0, blocking collectives: 61.6 us -> none
    pallas_call x1 -> x2, Pallas kernels: 4.79 us -> 44.7 us  [the longest x1 30.8 us: on_device(): pl.pallas_call(functools.partial(route_kernel, nv, length), in_specs=[vme...]
    all_to_all x2 -> x0, waiting for transfers between devices: 30.2 us -> none  [exchange(): return lax.all_to_all(blocks, 'context', 0, 0, tiled=True)]
    all_to_all x2 -> x0, starting transfers between devices: 11.7 us -> none  [exchange(): return lax.all_to_all(blocks, 'context', 0, 0, tiled=True)]
  transfers between devices with their start and end apart: 2 -> 0, of which waited for: 2 -> 0; matrix products, arithmetic and copies ran while one was open for 1% -> 0% of each run, Pallas kernels for 0% -> 0%
where the time goes in v1:
time: 76.1 us; the launch traced here: 75.3 us
  Pallas kernels  68.6 us (90%)
  local copies, waits for them, and re-layouts  5.36 us (7%)
    pallas_call x1, Pallas kernels, on_device(): pl.pallas_call(functools.partial(route_kernel, nv, length), in_specs=[vme...  30.8 us
    pallas_call x1, Pallas kernels, on_device(): pl.pallas_call(functools.partial(finish_kernel, nv), grid=(width // chunk...  17.3 us
    pallas_call x1, Pallas kernels, on_device(): pl.pallas_call(score_kernel, in_specs=[vmem], out_specs=vmem, out_shape=j...  13.9 us
    pallas_call x1, Pallas kernels, on_device(): pl.pallas_call(functools.partial(moments_kernel, nv), grid=(width // chun...  6.6 us

profile of v1, /device:TPU:0, one launch (start us, length us, event | category | flops | bytes accessed | tf_op | source)
XLA Modules:
  0.0 75.3 jit_solution(1808732484261653948)
XLA Ops:
  0.6 1.2 %dynamic_slice.14.alt_ref = s32[4]{0:T(128)} dynamic-slice(s32[64]{0:T(128)} %param.14, s32[]{:T(128)S(6)} %select_n.12), dynamic_slice_sizes={4} | dynamic-slice | bytes 36 | tf_op jit(solution)/shard_map/dynamic_slice | solution.py:279
  1.9 0.7 reshape.29
  2.6 0.1 convert_bitcast_fusion
  2.7 0.5 fusion.1.where_ref
  3.2 0.1 copy.15
  3.3 0.7 broadcast_in_dim.2.lag_ref
  4.0 1.4 %constant_dynamic-slice_fusion = (f32[16,512]{1,0:T(8,128)}, f32[16,512]{1,0:T(8,128)}) fusion(f32[16,8192]{1,0:T(8,128)} %residue_ref.1, s32[]{:T(128)S(6)} %select_n.13, f32[16,8192]{1,0:T(8,128)} %rate_ref.1), kind=kLoop, calls=%fused_computation.2 | loop fusion | bytes 131076 | tf_op jit(solution)/shard_map/dynamic_slice | solution.py:308
  5.4 6.6 %moments.1.mine_ref = f32[16,56,128]{2,1,0:T(8,128)} custom-call(s32[4]{0:T(128)} %fusion.1.where_ref, s32[4]{0:T(128)} %dynamic_slice.14.alt_ref, bf16[16,384]{1,0:T(8,128)(2,1)} %constant.33.clone.gm_ref, bf16[3,128,8192]{2,1,0:T(8,128)(2,1)} %bitcast.9, bf16[3,128,8192]{2,1,0:T(8,128)(2,1)} %bitcast.10, bf16[3,4,8192]{2,1,0:T(4,128)(2,1)} %bitcast.14), custom_call_target="tpu_custom_call" | custom-call | tf_op jit(solution)/shard_map/moments/pallas_call | solution.py:294
  12.0 30.8 %route.1.enter_ref = f32[16,80,128]{2,1,0:T(8,128)} custom-call(f32[4,16,128]{2,1,0:T(8,128)} %broadcast_in_dim.2.lag_ref, f32[16,56,128]{2,1,0:T(8,128)} %moments.1.mine_ref, f32[16,512]{1,0:T(8,128)} %get-tuple-element.12.rate_ref, f32[16,512]{1,0:T(8,128)} %get-tuple-element.11.residue_ref), custom_call_target="tpu_custom_call" | custom-call | tf_op jit(solution)/shard_map/route/pallas_call | solution.py:310
  42.7 17.3 %finish.1 = (bf16[128,8192]{1,0:T(8,128)(2,1)}, bf16[128,8192]{1,0:T(8,128)(2,1)}, f32[1,8192]{1,0:T(1,128)}) custom-call(s32[4]{0:T(128)} %fusion.1.where_ref, s32[4]{0:T(128)} %dynamic_slice.14.alt_ref, bf16[456,192]{1,0:T(8,128)(2,1)} %constant.34.clone.gb_ref, bf16[128,96]{1,0:T(8,128)(2,1)} %constant.35.clone.gx_ref, ...), custom_call_target="tpu_custom_call" | custom-call | tf_op jit(solution)/shard_map/finish/pallas_call | solution.py:335
  60.1 13.9 %score.1 = f32[4,128]{1,0:T(4,128)} custom-call(f32[16,4,128]{2,1,0:T(4,128)} %bitcast.17), custom_call_target="tpu_custom_call" | custom-call | tf_op jit(solution)/shard_map/score/pallas_call | solution.py:364
  74.0 1.2 %copy.17 = f32[512]{0:T(512)} copy(f32[512]{0:T(512)} %bitcast.18) | data formatting | bytes 4096
  (2 shorter events, 0.0 us)
